TPU v7x, 256 devices: a whole 4x4x8 slice. The times are simulated.
256 devices in a mesh: slab: 64 (over x, y_hi, z), pencil: 4 (over y_lo, core).
Axes of the slice: x: 4, y: 4 (y_hi: 2, y_lo: 2; y = y_hi * 2 + y_lo), z: 8, core: 2. Of those that a mesh axis runs over, the one named last changes fastest.
Arguments:
- fine_blocks: float32 [4, 65536, 3, 256], P('pencil', 'slab'), may hold values from -6 to 6
- owner_slab: int32 [4, 65536, 1], P('pencil', 'slab'), may hold values from 0 to 63; in each aligned block of 1024 rows (0 to 1023, 1024 to 2047, ..., all dimensions but the last counted through in order) at most 32 rows name the same one
- owner_row: int32 [4, 65536], P('pencil', 'slab'), may hold values from 0 to 2047
- valid_counts: int32 [4, 64], P('pencil', 'slab'), may hold values from 768 to 1024
- coarse_field: float32 [3, 256, 256, 1024], P(None, 'slab', 'pencil'), may hold values from -6 to 6
- active: int32 [256, 256, 1024], P('slab', 'pencil'), may hold values 0 or 1
Outputs:
- cleaned: float32 [3, 256, 256, 1024], P(None, 'slab', 'pencil')
Inputs may be any that keep to these rules, and one draw needn't show every extreme that they name: `owner_slab`: among the 1024 blocks of one holder (aligned runs along the second dimension) at most 32 name the same slab, and in some runs a slab is named by exactly 32 of them.
All inputs are finite; a program needn't handle non-finite values. No bound on the sum of `active` on one device may be relied on, other than what follows from the above.
Results may differ from a plain program's by a relative error of at most 0.00005.
Values sent between devices are 32-bit elements; how exact they have to be, the bound alone decides.
No kernel may reach another device: no remote copies, remote signals or barrier semaphores. Data moves between devices by JAX's collectives and lax.ppermute only.
A program may use at most 128 MiB of HBM per device.

v0:
```python
import jax
import jax.numpy as jnp
from jax import lax
from jax.experimental import pallas as pl
from jax.experimental.pallas import tpu as pltpu
from jax.sharding import PartitionSpec as P

F32, BF16 = jnp.float32, jnp.bfloat16
LANES = 128
SLOTS = 32
TAG_ROW = 3 * SLOTS
BOX_ROWS = TAG_ROW + 1
PACK_GROUP = 16
PACK_BYTES = 60 << 20
OUTER_BYTES = 24 << 20
INNER_BYTES = 16 << 20
DIVERGE_BYTES = 16 << 20
CORRECT_BYTES = 24 << 20


def iota(shape, dim):
    return lax.broadcasted_iota(jnp.int32, shape, dim)


def halves(value):
    high = value.astype(BF16)
    return high, (value - high.astype(F32)).astype(BF16)


def dot(left, right):
    return jnp.dot(left, right, preferred_element_type=F32)


def dot_rows(left, right):
    return lax.dot_general(left, right, (((1,), (1,)), ((), ())), preferred_element_type=F32)


def hot(mask):
    return jnp.where(mask, 1.0, 0.0)


def pack_kernel(valid_counts, slab, row, fine, out, coarse, chosen, box, arrived, in_sems, out_sems):
    count_held = slab.shape[1]
    slab_count = chosen.shape[0] // SLOTS
    group = min(PACK_GROUP, slab_count)
    valid = valid_counts[0, 0]
    lane_base = lax.axis_index("slab") % 4 * SLOTS
    loads = [
        pltpu.make_async_copy(fine.at[part], arrived.at[part], in_sems.at[part]) for part in range(3)
    ]
    for load in loads:
        load.start()
    piece = min(LANES, count_held)
    before = hot(iota((piece, piece), 0) < iota((piece, piece), 1)).astype(BF16)
    pieces = range(0, count_held, piece)
    named_all, earlier_all, rank_all, running = [], [], [], jnp.zeros((slab_count, 1), F32)
    for start in pieces:
        live = iota((1, piece), 1) + start < valid
        target = jnp.where(live, slab[:, start : start + piece], -1)
        named = hot(iota((slab_count, piece), 0) == target)
        named_all.append(named)
    for named in named_all:
        earlier_all.append(dot(named.astype(BF16), before) + running)
        running = running + jnp.sum(named, axis=1, keepdims=True)
    table = jnp.zeros((slab_count, LANES), F32)
    for start, named, earlier in zip(pieces, named_all, earlier_all):
        lanes = slice(start, start + piece)
        rank = jnp.sum(named * earlier, axis=0, keepdims=True).astype(jnp.int32)
        rank_all.append(hot(iota((SLOTS, piece), 0) == rank).astype(BF16))
        tag = row[:, lanes] + 1
        place = hot(iota((LANES, piece), 0) == rank + lane_base).astype(BF16)
        upper = (named * (tag // 64).astype(F32)).astype(BF16)
        lower = (named * (tag % 64).astype(F32)).astype(BF16)
        table = table + dot_rows(upper, place) * 64.0 + dot_rows(lower, place)
    rank16 = jnp.concatenate(rank_all, axis=1)
    named16 = jnp.concatenate([named.astype(BF16) for named in named_all], axis=1)
    for g in range(slab_count):
        chosen[g * SLOTS : (g + 1) * SLOTS, :] = rank16 * named16[g : g + 1, :]
        start = g * BOX_ROWS + TAG_ROW
        box[start : start + 1, :] = table[g : g + 1]
    pick = jnp.where(
        iota((2 * LANES, LANES), 0) // 2 == iota((2 * LANES, LANES), 1), 0.5, 0.0
    ).astype(BF16)
    chunk = min(256, count_held)
    stores = []
    for part in range(3):
        loads[part].wait()
        for start in range(0, count_held, chunk):
            rows = slice(start, start + chunk)
            high, low = halves(arrived[part, rows, :])
            mean_high, mean_low = halves(dot(high, pick) + dot(low, pick))
            coarse[part, rows, 0:LANES] = mean_high
            coarse[part, rows, LANES:] = mean_low
        for first in range(0, slab_count, group):
            both = dot(chosen[first * SLOTS : (first + group) * SLOTS, :], coarse[part])
            rows = both[:, :LANES] + both[:, LANES:]
            for g in range(group):
                start = (first + g) * BOX_ROWS + part * SLOTS
                box[start : start + SLOTS, :] = rows[g * SLOTS : (g + 1) * SLOTS]
            if part == 2:
                at = slice(first * BOX_ROWS, (first + group) * BOX_ROWS)
                index = first // group
                store = pltpu.make_async_copy(box.at[at], out.at[at], out_sems.at[index])
                store.start()
                stores.append(store)
    for store in stores:
        store.wait()


def pack(valid_counts, slab, row, fine, slab_count):
    count_held = slab.shape[1]
    vmem = pl.BlockSpec(memory_space=pltpu.VMEM)
    hbm = pl.BlockSpec(memory_space=pltpu.HBM)
    return pl.pallas_call(
        pack_kernel,
        in_specs=[pl.BlockSpec(memory_space=pltpu.SMEM), vmem, vmem, hbm],
        out_specs=hbm,
        out_shape=jax.ShapeDtypeStruct((slab_count * BOX_ROWS, LANES), F32),
        scratch_shapes=[
            pltpu.VMEM((3, count_held, 2 * LANES), BF16),
            pltpu.VMEM((slab_count * SLOTS, count_held), BF16),
            pltpu.VMEM((slab_count * BOX_ROWS, LANES), F32),
            pltpu.VMEM((3, count_held, 2 * LANES), F32),
            pltpu.SemaphoreType.DMA((3,)),
            pltpu.SemaphoreType.DMA((max(1, slab_count // PACK_GROUP),)),
        ],
        compiler_params=pltpu.CompilerParams(vmem_limit_bytes=PACK_BYTES),
        name="pack",
    )(valid_counts, slab, row, fine)


OUTER, INNER = (0, 1, 6, 7), (2, 3, 4, 5)


def rows_of(tiles, tile):
    return slice(tiles.index(tile) * 8, tiles.index(tile) * 8 + 8)


def tile_of(outer, inner, part, z, tile):
    if tile in OUTER:
        return outer[part, z, rows_of(OUTER, tile), :]
    return inner[part, z, rows_of(INNER, tile), :]


def divergence_tile(outer, inner, z, tile):
    depth_z, width_x = outer.shape[1], outer.shape[3]
    face_x, face_y, face_z = (tile_of(outer, inner, part, z, tile) for part in range(3))
    above_z = tile_of(outer, inner, 2, z + 1, tile) if z + 1 < depth_z else 0.0
    next_x = jnp.where(
        iota((8, width_x), 1) == width_x - 1, 0.0, pltpu.roll(face_x, width_x - 1, 1)
    )
    after = tile_of(outer, inner, 1, z, tile + 1)[0:1] if tile < 7 else 0.0
    next_y = jnp.where(iota((8, width_x), 0) == 7, after, pltpu.roll(face_y, 7, 0))
    return (next_x - face_x) + (next_y - face_y) + (above_z - face_z)


def put_plane(low_planes, high_planes, depth_z, z, rows, value):
    if z > depth_z - 4:
        low_planes[z - depth_z + 3, rows, :] = value
    if z < 2:
        high_planes[z, rows, :] = value


def sum_tiles(tiles, rows16, line_hot, tile_hot, number, base, field):
    depth_z, depth_y, width_x = base.shape[1:]
    for low_z in range(0, depth_z, 2):
        pairs = [(z, tile) for z in (low_z, low_z + 1) for tile in tiles]
        line16 = line_hot[...]
        chosen = jnp.concatenate(
            [
                line16 * tile_hot[z * 8 + tile : z * 8 + tile + 1, :]
                for z, tile in pairs
            ],
            axis=0,
        )
        both = dot(chosen, rows16[...])
        for at, (z, tile) in enumerate(pairs):
            found = number[z * 8 + tile]
            scale = 1.0 / jnp.maximum(found, 1.0)
            rows = slice(at * 64, at * 64 + 64)
            from_rows, to_rows = slice(tile * 8, tile * 8 + 8), rows_of(tiles, tile)
            for part in range(3):
                totals = both[rows, part * LANES : (part + 1) * LANES]
                totals = totals + both[rows, (3 + part) * LANES : (4 + part) * LANES]
                averaged = totals * scale
                for xb in range(width_x // LANES):
                    xs, at8 = slice(xb * LANES, (xb + 1) * LANES), slice(xb * 8, xb * 8 + 8)
                    field[part, z, to_rows, xs] = jnp.where(
                        found[at8] > 0.5, averaged[at8], base[part, z, from_rows, xs]
                    )


def outer_kernel(
    box, base, field, low_rows, high_rows, rows16, line_hot, tile_hot, number
):
    slab_count = box.shape[0] // BOX_ROWS
    depth_z = base.shape[1]
    width = 3 * LANES
    tag_rows = [box[i * BOX_ROWS + TAG_ROW : (i + 1) * BOX_ROWS, :] for i in range(slab_count)]
    sums = [sum(tag_rows[i + 1 : i + 4], tag_rows[i]) for i in range(0, slab_count, 4)]
    tags = jnp.concatenate(sums, axis=0).astype(jnp.int32) - 1
    tiles, within = tags >> 6, tags & 63
    order = iota((64, LANES), 0)
    order = order % 8 * 8 + order // 8
    counts = jnp.zeros((64, tile_hot.shape[0]), F32)
    for g in range(slab_count // 4):
        lanes = slice(g * LANES, (g + 1) * LANES)
        line16 = hot(within[g : g + 1, :] == order).astype(BF16)
        tile16 = hot(tiles[g : g + 1, :] == iota((tile_hot.shape[0], LANES), 0)).astype(BF16)
        line_hot[:, lanes] = line16
        tile_hot[:, lanes] = tile16
        counts = counts + dot_rows(line16, tile16)
    for tile in range(tile_hot.shape[0]):
        number[tile] = jnp.broadcast_to(counts[:, tile : tile + 1], (64, LANES))
    for part in range(3):
        for i in range(slab_count):
            start = i * BOX_ROWS + part * SLOTS
            high, low = halves(box[start : start + SLOTS, :])
            rows = slice(i * SLOTS, (i + 1) * SLOTS)
            rows16[rows, part * LANES : (part + 1) * LANES] = high
            rows16[rows, width + part * LANES : width + (part + 1) * LANES] = low
    sum_tiles(OUTER, rows16, line_hot, tile_hot, number, base, field)
    for z in range(depth_z):
        high_rows[3 * z : 3 * z + 2, :] = divergence_tile(field, None, z, 0)[0:2]
        high_rows[3 * z + 2 : 3 * z + 3, :] = tile_of(field, None, 1, z, 0)[0:1]
        low_rows[3 * z : 3 * z + 3, :] = divergence_tile(field, None, z, 7)[5:8]
    end = 3 * depth_z
    low_rows[end : end + 3, :] = tile_of(field, None, 2, 0, 7)[5:8]
    high_rows[end : end + 3, :] = tile_of(field, None, 2, 0, 0)[0:3]


def inner_kernel(rows16, line_hot, tile_hot, number, base, field):
    sum_tiles(INNER, rows16, line_hot, tile_hot, number, base, field)


def vmem_call(kernel, shapes, limit, name):
    vmem = pl.BlockSpec(memory_space=pltpu.VMEM)
    return lambda *operands: pl.pallas_call(
        kernel,
        in_specs=[vmem] * len(operands),
        out_specs=[vmem] * len(shapes),
        out_shape=[jax.ShapeDtypeStruct(dims, dtype) for dims, dtype in shapes],
        compiler_params=pltpu.CompilerParams(vmem_limit_bytes=limit),
        name=name,
    )(*operands)


def sum_outer(box, base):
    slots = box.shape[0] // BOX_ROWS * SLOTS
    _, depth_z, depth_y, width_x = base.shape
    line_count = -(-3 * (depth_z + 1) // 8) * 8
    shapes = [
        ((3, depth_z, 8 * len(OUTER), width_x), F32),
        ((line_count, width_x), F32),
        ((line_count, width_x), F32),
        ((slots, 6 * LANES), BF16),
        ((64, slots), BF16),
        ((depth_z * depth_y // 8, slots), BF16),
        ((depth_z * depth_y // 8, 64, LANES), F32),
    ]
    return vmem_call(outer_kernel, shapes, OUTER_BYTES, "sum_outer")(box, base)


def sum_inner(tables, base):
    _, depth_z, _, width_x = base.shape
    shapes = [((3, depth_z, 8 * len(INNER), width_x), F32)]
    return vmem_call(inner_kernel, shapes, INNER_BYTES, "sum_inner")(*tables, base)[0]


def diverge_kernel(outer, inner, own, below, above, partial, beside, low_planes, high_planes):
    depth_z = outer.shape[1]
    for z in range(depth_z):
        for tile in range(8):
            value = divergence_tile(outer, inner, z, tile)
            if tile == 7:
                face = above[3 * z + 2 : 3 * z + 3, :]
                value = value + jnp.where(iota(value.shape, 0) == 7, face, 0.0)
            rows = slice(tile * 8, tile * 8 + 8)
            partial[z, rows, :] = value
            put_plane(low_planes, high_planes, depth_z, z, rows, value)
            if z == 0:
                high_planes[2, rows, :] = tile_of(outer, inner, 2, 0, tile)
    ext = slice(64, 72)
    for z in range(depth_z + 1):
        beside[z, 0:3, :] = above[3 * z : 3 * z + 3, :]
        beside[z, 3:5, :] = jnp.zeros_like(beside[z, 3:5, :])
        under = below[3 * z : 3 * z + 3, :]
        if z < depth_z:
            face = own[3 * z + 2 : 3 * z + 3, :]
            under = under + jnp.where(iota(under.shape, 0) == 2, face, 0.0)
        beside[z, 5:8, :] = under
        if z < depth_z:
            put_plane(low_planes, high_planes, depth_z, z, ext, beside[z])
        else:
            high_planes[2, ext, :] = beside[z]


def diverge(outer, inner, own, below, above):
    depth_z, width_x = outer.shape[1], outer.shape[3]
    shapes = [((depth_z, 64, width_x), F32), ((depth_z + 1, 8, width_x), F32)]
    shapes += [((3, 72, width_x), F32)] * 2
    return vmem_call(diverge_kernel, shapes, DIVERGE_BYTES, "diverge")(
        outer, inner, own, below, above
    )


def correct_kernel(
    outer, inner, partial, beside, below, above, active,
    out, first, second, third, active_here, out_here, in_sem, out_sems
):
    depth_z, depth_y, width_x = partial.shape
    planes = depth_z + 5
    tiles = depth_y // 8 + 2
    line = iota((8, width_x), 0)
    column = iota((8, width_x), 1)
    slab_at, band_at = lax.axis_index("slab"), lax.axis_index("pencil")
    has_low_z = jnp.where(slab_at > 0, 1.0, 0.0)
    has_high_z = jnp.where(slab_at < lax.axis_size("slab") - 1, 1.0, 0.0)
    has_low_y = jnp.where(band_at > 0, 1.0, 0.0)
    has_high_y = jnp.where(band_at < lax.axis_size("pencil") - 1, 1.0, 0.0)
    load = pltpu.make_async_copy(active, active_here, in_sem)
    load.start()
    sixth = 1.0 / 6.0

    def z_scale(p):
        return has_low_z if p < 3 else (has_high_z if p >= depth_z + 3 else 1.0)

    def y_scale(t):
        return has_low_y if t == 0 else (has_high_y if t == tiles - 1 else 1.0)

    def fill(p):
        z = p - 3
        for t in range(tiles):
            inside = 0 < t < tiles - 1
            rows = slice(t * 8 - 8, t * 8) if inside else slice(depth_y, depth_y + 8)
            if z < 0:
                value = below[p, rows, :]
                if z == -1:
                    value = value + (tile_of(outer, inner, 2, 0, t - 1) if inside else beside[depth_z])
            elif z < depth_z:
                value = partial[z, rows, :] if inside else beside[z]
                if z == depth_z - 1:
                    value = value + above[2, rows, :]
            else:
                value = above[z - depth_z, rows, :]
            first[p, t * 8 : t * 8 + 8, :] = value * (-sixth * z_scale(p) * y_scale(t))

    def around(source, p, t):
        centre = source[p, t * 8 : t * 8 + 8, :]
        total = source[p - 1, t * 8 : t * 8 + 8, :] + source[p + 1, t * 8 : t * 8 + 8, :]
        lower = source[p, t * 8 - 1 : t * 8, :] if t > 0 else 0.0
        upper = source[p, t * 8 + 8 : t * 8 + 9, :] if t < tiles - 1 else 0.0
        total = total + jnp.where(line == 0, lower, pltpu.roll(centre, 1, 0))
        total = total + jnp.where(line == 7, upper, pltpu.roll(centre, 7, 0))
        total = total + jnp.where(column == 0, 0.0, pltpu.roll(centre, 1, 1))
        return total + jnp.where(column == width_x - 1, 0.0, pltpu.roll(centre, width_x - 1, 1))

    def sweep(source, target, p, count):
        for t in range(count):
            value = around(source, p, t) * sixth + first[p, t * 8 : t * 8 + 8, :]
            scaled = not (3 <= p < depth_z + 3 and 0 < t < tiles - 1)
            target[p, t * 8 : t * 8 + 8, :] = value * (z_scale(p) * y_scale(t)) if scaled else value

    def finish(z):
        p = z + 3
        for t in range(1, tiles - 1):
            ys, rows = slice(t * 8 - 8, t * 8), slice(t * 8, t * 8 + 8)
            mask = active_here[z, ys, :].astype(F32)
            centre = third[p, rows, :]
            left = jnp.where(column == 0, 0.0, pltpu.roll(centre, 1, 1))
            lower = jnp.where(line == 0, third[p, t * 8 - 1 : t * 8, :], pltpu.roll(centre, 1, 0))
            under = third[p - 1, rows, :]
            for part, other in enumerate((left, lower, under)):
                face = tile_of(outer, inner, part, z, t - 1)
                out_here[part, z, ys, :] = face - mask * (centre - other)
        store = pltpu.make_async_copy(out_here.at[:, z], out.at[:, z], out_sems.at[z])
        store.start()
        return store

    fill(0)
    fill(1)
    load.wait()
    stores = []
    for p in range(1, planes - 1):
        fill(p + 1)
        sweep(first, second, p, tiles)
        if p > 2:
            sweep(second, third, p - 1, tiles - 1)
        if p > 3:
            stores.append(finish(p - 4))
    for store in stores:
        store.wait()


def correct(outer, inner, partial, beside, below, above, active):
    depth_z, depth_y, width_x = partial.shape
    extended = pltpu.VMEM((depth_z + 5, depth_y + 16, width_x), F32)
    vmem = pl.BlockSpec(memory_space=pltpu.VMEM)
    hbm = pl.BlockSpec(memory_space=pltpu.HBM)
    out_dims = (3, depth_z, depth_y, width_x)
    return pl.pallas_call(
        correct_kernel,
        in_specs=[vmem] * 6 + [hbm],
        out_specs=hbm,
        out_shape=jax.ShapeDtypeStruct(out_dims, F32),
        scratch_shapes=[extended] * 3
        + [
            pltpu.VMEM(active.shape, active.dtype),
            pltpu.VMEM(out_dims, F32),
            pltpu.SemaphoreType.DMA,
            pltpu.SemaphoreType.DMA((depth_z,)),
        ],
        compiler_params=pltpu.CompilerParams(vmem_limit_bytes=CORRECT_BYTES),
        name="correct",
    )(outer, inner, partial, beside, below, above, active)


def moved(value, axis, steps):
    count = lax.axis_size(axis)
    pairs = [(i, i + steps) for i in range(count) if 0 <= i + steps < count]
    return lax.ppermute(value, axis, pairs)


def shards(fine_blocks, owner_slab, owner_row, valid_counts, coarse_field, active):
    slab_count = lax.axis_size("slab")
    count_held = fine_blocks.shape[1]
    fine = fine_blocks[0].transpose(1, 0, 2)
    out_box = pack(valid_counts, owner_slab.reshape(1, count_held), owner_row, fine, slab_count)
    out_box = out_box.reshape(slab_count, BOX_ROWS, 1, LANES)
    box = lax.all_to_all(out_box, "slab", split_axis=0, concat_axis=0, tiled=True)
    box = box.reshape(slab_count * BOX_ROWS, LANES)
    outer, low_rows, high_rows, *tables = sum_outer(box, coarse_field)
    rows_below = moved(low_rows, "pencil", 1)
    rows_above = moved(high_rows, "pencil", -1)
    inner = sum_inner(tables, coarse_field)
    partial, beside, low_planes, high_planes = diverge(
        outer, inner, high_rows, rows_below, rows_above
    )
    below = moved(low_planes, "slab", 1)
    above = moved(high_planes, "slab", -1)
    return correct(outer, inner, partial, beside, below, above, active)


def solution(mesh):
    in_specs = (
        P("pencil", "slab", None, None),
        P("pencil", "slab", None),
        P("pencil", "slab"),
        P("pencil", "slab"),
        P(None, "slab", "pencil", None),
        P("slab", "pencil", None),
    )
    out_specs = P(None, "slab", "pencil", None)
    return jax.shard_map(shards, mesh=mesh, in_specs=in_specs, out_specs=out_specs, check_vma=False)
```

profile of v0, /device:TPU:3, one launch (start us, length us, event | category | flops | bytes accessed | tf_op | source)
XLA Modules:
  0.0 143.7 jit_solution(2165652994815994644)
XLA Ops:
  0.7 7.7 %pack.1 = f32[6208,128]{1,0:T(8,128)} custom-call(s32[1,1]{1,0:T(1,128)S(6)} %copy.8.valid_counts, s32[1,1024]{1,0:T(1,128)} %bitcast.9, s32[1,1024]{1,0:T(1,128)} %row.1, f32[3,1024,256]{2,1,0:T(8,128)} %bitcast.8), custom_call_target="tpu_custom_call" | custom-call | tf_op jit(solution)/shard_map/pack/pallas_call | solution.py:114
  8.3 0.0 copy-start
  8.3 86.9 %all_to_all.5 = f32[64,97,1,128]{3,2,1,0:T(1,128)S(1)} all-to-all(f32[64,97,1,128]{3,2,1,0:T(1,128)} %bitcast.7), channel_id=1, replica_groups=mesh['slab'=64,'pencil'=4] {'slab'}, dimensions={0} | all-to-all | bytes 6356992 | tf_op jit(solution)/shard_map/all_to_all | solution.py:430
  95.2 0.0 copy-done
  95.2 3.9 %sum_outer.1 = (f32[3,4,32,1024]{3,2,1,0:T(8,128)S(1)}, f32[16,1024]{1,0:T(8,128)S(1)}, f32[16,1024]{1,0:T(8,128)S(1)}, bf16[2048,768]{1,0:T(8,128)(2,1)S(1)}, b...) custom-call(f32[6208,128]{1,0:T(8,128)S(1)} %bitcast.6, ...), custom_call_target="tpu_custom_call" | custom-call | tf_op jit(solution)/shard_map/sum_outer/pallas_call | solution.py:238
  99.1 6.1 %collective-permute-start = (f32[16,1024]{1,0:T(8,128)S(1)}, f32[16,1024]{1,0:T(8,128)S(1)}, u32[]{:S(2)}, u32[]{:S(2)}) collective-permute-start(f32[16,1024]{1,0:T(8,128)S(1)} %get-tuple-element.22), channel_id=1, source_target_pairs={{0,1},{1,2},{2,3},{4,5},{5,6},{6,7},{8,9},{9,10},{10,11},{12,13},{... | collective-permute-start | bytes 196616 | tf_op jit(solution)/shard_map/ppermute | solution.py:421
  105.2 1.9 %collective-permute-start.1 = (f32[16,1024]{1,0:T(8,128)S(1)}, f32[16,1024]{1,0:T(8,128)S(1)}, u32[]{:S(2)}, u32[]{:S(2)}) collective-permute-start(f32[16,1024]{1,0:T(8,128)S(1)} %get-tuple-element.21.own), channel_id=1, source_target_pairs={{1,0},{2,1},{3,2},{5,4},{6,5},{7,6},{9,8},{10,9},{11,10},{13,12},{... | collective-permute-start | bytes 196616 | tf_op jit(solution)/shard_map/ppermute | solution.py:421
  107.1 3.4 %sum_inner.1.inner = f32[3,4,32,1024]{3,2,1,0:T(8,128)S(1)} custom-call(bf16[2048,768]{1,0:T(8,128)(2,1)S(1)} %get-tuple-element.17.rows16, bf16[64,2048]{1,0:T(8,128)(2,1)S(1)} %get-tuple-element.18.line_hot, bf16[32,2048]{1,0:T(8,128)(2,1)S(1)} %get-tuple-element.19.tile_hot, f32[32,64,128]{2,1,0:T(8,128)S(1)} %get-tuple-element.20.number, ...), custom_call_target="tpu_custom_call" | custom-call | tf_op jit(solution)/shard_map/sum_inner/pallas_call | solution.py:238
  110.6 0.0 copy-start.1
  110.6 0.0 collective-permute-done.below
  110.6 0.2 collective-permute-done.1.above
  110.8 0.6 diverge.1
  111.4 2.9 %collective-permute-start.2 = (f32[3,72,1024]{2,1,0:T(8,128)S(1)}, f32[3,72,1024]{2,1,0:T(8,128)S(1)}, u32[]{:S(2)}, u32[]{:S(2)}) collective-permute-start(f32[3,72,1024]{2,1,0:T(8,128)S(1)} %get-tuple-element.25), channel_id=1, source_target_pairs={{0,4},{4,8},{8,12},{12,16},{16,20},{20,24},{24,28},{28,32},{32,36}... | collective-permute-start | bytes 2654216 | tf_op jit(solution)/shard_map/ppermute | solution.py:421
  114.3 7.1 %collective-permute-start.3 = (f32[3,72,1024]{2,1,0:T(8,128)S(1)}, f32[3,72,1024]{2,1,0:T(8,128)S(1)}, u32[]{:S(2)}, u32[]{:S(2)}) collective-permute-start(f32[3,72,1024]{2,1,0:T(8,128)S(1)} %get-tuple-element.26), channel_id=1, source_target_pairs={{4,0},{8,4},{12,8},{16,12},{20,16},{24,20},{28,24},{32,28},{36,32}... | collective-permute-start | bytes 2654216 | tf_op jit(solution)/shard_map/ppermute | solution.py:421
  121.4 16.5 %collective-permute-done.2.below = f32[3,72,1024]{2,1,0:T(8,128)S(1)} collective-permute-done((f32[3,72,1024]{2,1,0:T(8,128)S(1)}, f32[3,72,1024]{2,1,0:T(8,128)S(1)}, u32[]{:S(2)}, u32[]{:S(2)}) %collective-permute-start.2) | collective-permute-done | bytes 884768 | tf_op jit(solution)/shard_map/ppermute | solution.py:421
  137.9 1.8 %collective-permute-done.3.above = f32[3,72,1024]{2,1,0:T(8,128)S(1)} collective-permute-done((f32[3,72,1024]{2,1,0:T(8,128)S(1)}, f32[3,72,1024]{2,1,0:T(8,128)S(1)}, u32[]{:S(2)}, u32[]{:S(2)}) %collective-permute-start.3) | collective-permute-done | bytes 884768 | tf_op jit(solution)/shard_map/ppermute | solution.py:421
  139.7 0.0 copy-done.1
  139.7 3.9 %correct.1 = f32[3,4,64,1024]{3,2,1,0:T(8,128)} custom-call(f32[3,4,32,1024]{3,2,1,0:T(8,128)S(1)} %get-tuple-element.16.outer, f32[3,4,32,1024]{3,2,1,0:T(8,128)S(1)} %sum_inner.1.inner, f32[4,64,1024]{2,1,0:T(8,128)S(1)} %get-tuple-element.23.partial, f32[5,8,1024]{2,1,0:T(8,128)S(1)} %get-tuple-element.24.beside, ...), custom_call_target="tpu_custom_call" | custom-call | tf_op jit(solution)/shard_map/correct/pallas_call | solution.py:401
Async XLA Ops:
  8.3 86.9 %copy-start = (f32[3,4,64,1024]{3,2,1,0:T(8,128)S(1)}, f32[3,4,64,1024]{3,2,1,0:T(8,128)}, u32[]{:S(2)}) copy-start(f32[3,4,64,1024]{3,2,1,0:T(8,128)} %base.3) | copy-start | bytes 9437188
  99.1 11.5 %collective-permute-start = (f32[16,1024]{1,0:T(8,128)S(1)}, f32[16,1024]{1,0:T(8,128)S(1)}, u32[]{:S(2)}, u32[]{:S(2)}) collective-permute-start(f32[16,1024]{1,0:T(8,128)S(1)} %get-tuple-element.22), channel_id=1, source_target_pairs={{0,1},{1,2},{2,3},{4,5},{5,6},{6,7},{8,9},{9,10},{10,11},{12,13},{... | collective-permute-start | bytes 196616 | tf_op jit(solution)/shard_map/ppermute | solution.py:421
  105.2 5.6 %collective-permute-start.1 = (f32[16,1024]{1,0:T(8,128)S(1)}, f32[16,1024]{1,0:T(8,128)S(1)}, u32[]{:S(2)}, u32[]{:S(2)}) collective-permute-start(f32[16,1024]{1,0:T(8,128)S(1)} %get-tuple-element.21.own), channel_id=1, source_target_pairs={{1,0},{2,1},{3,2},{5,4},{6,5},{7,6},{9,8},{10,9},{11,10},{13,12},{... | collective-permute-start | bytes 196616 | tf_op jit(solution)/shard_map/ppermute | solution.py:421
  110.6 29.1 %copy-start.1 = (s32[4,64,1024]{2,1,0:T(8,128)S(1)}, s32[4,64,1024]{2,1,0:T(8,128)}, u32[]{:S(2)}) copy-start(s32[4,64,1024]{2,1,0:T(8,128)} %active.1) | copy-start | bytes 3145732
  111.4 26.5 %collective-permute-start.2 = (f32[3,72,1024]{2,1,0:T(8,128)S(1)}, f32[3,72,1024]{2,1,0:T(8,128)S(1)}, u32[]{:S(2)}, u32[]{:S(2)}) collective-permute-start(f32[3,72,1024]{2,1,0:T(8,128)S(1)} %get-tuple-element.25), channel_id=1, source_target_pairs={{0,4},{4,8},{8,12},{12,16},{16,20},{20,24},{24,28},{28,32},{32,36}... | collective-permute-start | bytes 2654216 | tf_op jit(solution)/shard_map/ppermute | solution.py:421
  114.3 25.4 %collective-permute-start.3 = (f32[3,72,1024]{2,1,0:T(8,128)S(1)}, f32[3,72,1024]{2,1,0:T(8,128)S(1)}, u32[]{:S(2)}, u32[]{:S(2)}) collective-permute-start(f32[3,72,1024]{2,1,0:T(8,128)S(1)} %get-tuple-element.26), channel_id=1, source_target_pairs={{4,0},{8,4},{12,8},{16,12},{20,16},{24,20},{28,24},{32,28},{36,32}... | collective-permute-start | bytes 2654216 | tf_op jit(solution)/shard_map/ppermute | solution.py:421
where the time goes:
time: 144 us
  blocking collectives  86.9 us (60%)
  Pallas kernels  19.5 us (14%)
  waiting for transfers between devices  18.5 us (13%)
  starting transfers between devices  18 us (12%)
    all_to_all x1, blocking collectives, shards(): lax.all_to_all(out_box, 'slab', split_axis=0, concat_axis=0, tiled=True)  86.9 us
    ppermute x4, waiting for transfers between devices, moved(): return lax.ppermute(value, axis, pairs)  18.5 us
    ppermute x4, starting transfers between devices, moved(): return lax.ppermute(value, axis, pairs)  18 us
    pallas_call x3, Pallas kernels, vmem_call(): pl.pallas_call(kernel, in_specs=[vmem] * len(operands), out_specs=[vmem]...  7.91 us
    pallas_call x1, Pallas kernels, pack(): pl.pallas_call(pack_kernel, in_specs=[pl.BlockSpec(memory_space=pltpu.SME...  7.68 us
    pallas_call x1, Pallas kernels, correct(): pl.pallas_call(correct_kernel, in_specs=[vmem] * 6 + [hbm], out_specs=hbm...  3.89 us
  transfers between devices with their start and end apart: 4, of which 3 were waited for; matrix products, arithmetic and copies ran while one was open for 0% of the time, Pallas kernels for 2%

commit v1 on v0

--- a/solution.py
+++ b/solution.py
@@ -130,6 +130,7 @@
 
 
 OUTER, INNER = (0, 1, 6, 7), (2, 3, 4, 5)
+EARLY, LATE = (0, 6, 7), (1, 2, 3, 4, 5)
 
 
 def rows_of(tiles, tile):
@@ -191,7 +192,7 @@
 
 
 def outer_kernel(
-    box, base, field, low_rows, high_rows, rows16, line_hot, tile_hot, number
+    box, base, field, low_rows, high_rows, low_planes, high_planes, rows16, line_hot, tile_hot, number
 ):
     slab_count = box.shape[0] // BOX_ROWS
     depth_z = base.shape[1]
@@ -221,9 +222,16 @@
             rows16[rows, width + part * LANES : width + (part + 1) * LANES] = low
     sum_tiles(OUTER, rows16, line_hot, tile_hot, number, base, field)
     for z in range(depth_z):
-        high_rows[3 * z : 3 * z + 2, :] = divergence_tile(field, None, z, 0)[0:2]
-        high_rows[3 * z + 2 : 3 * z + 3, :] = tile_of(field, None, 1, z, 0)[0:1]
-        low_rows[3 * z : 3 * z + 3, :] = divergence_tile(field, None, z, 7)[5:8]
+        for tile in EARLY:
+            value = divergence_tile(field, None, z, tile)
+            put_plane(low_planes, high_planes, depth_z, z, rows_of(EARLY, tile), value)
+            if z == 0:
+                high_planes[2, rows_of(EARLY, tile), :] = tile_of(field, None, 2, 0, tile)
+            if tile == 0:
+                high_rows[3 * z : 3 * z + 2, :] = value[0:2]
+                high_rows[3 * z + 2 : 3 * z + 3, :] = tile_of(field, None, 1, z, 0)[0:1]
+            if tile == 7:
+                low_rows[3 * z : 3 * z + 3, :] = value[5:8]
     end = 3 * depth_z
     low_rows[end : end + 3, :] = tile_of(field, None, 2, 0, 7)[5:8]
     high_rows[end : end + 3, :] = tile_of(field, None, 2, 0, 0)[0:3]
@@ -253,6 +261,8 @@
         ((3, depth_z, 8 * len(OUTER), width_x), F32),
         ((line_count, width_x), F32),
         ((line_count, width_x), F32),
+        ((3, 8 * len(EARLY), width_x), F32),
+        ((3, 8 * len(EARLY), width_x), F32),
         ((slots, 6 * LANES), BF16),
         ((64, slots), BF16),
         ((depth_z * depth_y // 8, slots), BF16),
@@ -267,7 +277,10 @@
     return vmem_call(inner_kernel, shapes, INNER_BYTES, "sum_inner")(*tables, base)[0]
 
 
-def diverge_kernel(outer, inner, own, below, above, partial, beside, low_planes, high_planes):
+def diverge_kernel(
+    outer, inner, own, below, above, below_early, above_early, partial, beside, low_planes, high_planes
+):
+    del below_early, above_early
     depth_z = outer.shape[1]
     for z in range(depth_z):
         for tile in range(8):
@@ -275,12 +288,12 @@
             if tile == 7:
                 face = above[3 * z + 2 : 3 * z + 3, :]
                 value = value + jnp.where(iota(value.shape, 0) == 7, face, 0.0)
-            rows = slice(tile * 8, tile * 8 + 8)
-            partial[z, rows, :] = value
-            put_plane(low_planes, high_planes, depth_z, z, rows, value)
-            if z == 0:
-                high_planes[2, rows, :] = tile_of(outer, inner, 2, 0, tile)
-    ext = slice(64, 72)
+            partial[z, tile * 8 : tile * 8 + 8, :] = value
+            if tile in LATE:
+                put_plane(low_planes, high_planes, depth_z, z, rows_of(LATE, tile), value)
+                if z == 0:
+                    high_planes[2, rows_of(LATE, tile), :] = tile_of(outer, inner, 2, 0, tile)
+    ext = slice(8 * len(LATE), 8 * len(LATE) + 8)
     for z in range(depth_z + 1):
         beside[z, 0:3, :] = above[3 * z : 3 * z + 3, :]
         beside[z, 3:5, :] = jnp.zeros_like(beside[z, 3:5, :])
@@ -295,17 +308,23 @@
             high_planes[2, ext, :] = beside[z]
 
 
-def diverge(outer, inner, own, below, above):
+def diverge(outer, inner, own, below, above, early):
     depth_z, width_x = outer.shape[1], outer.shape[3]
-    shapes = [((depth_z, 64, width_x), F32), ((depth_z + 1, 8, width_x), F32)]
-    shapes += [((3, 72, width_x), F32)] * 2
-    return vmem_call(diverge_kernel, shapes, DIVERGE_BYTES, "diverge")(
-        outer, inner, own, below, above
-    )
+    shape = lambda *dims: jax.ShapeDtypeStruct(dims, F32)
+    vmem = pl.BlockSpec(memory_space=pltpu.VMEM)
+    return pl.pallas_call(
+        diverge_kernel,
+        in_specs=[vmem] * 5 + [pl.BlockSpec(memory_space=pl.ANY)] * 2,
+        out_specs=[vmem] * 4,
+        out_shape=[shape(depth_z, 64, width_x), shape(depth_z + 1, 8, width_x)]
+        + [shape(3, 8 * len(LATE) + 8, width_x)] * 2,
+        compiler_params=pltpu.CompilerParams(vmem_limit_bytes=DIVERGE_BYTES),
+        name="diverge",
+    )(outer, inner, own, below, above, *early)
 
 
 def correct_kernel(
-    outer, inner, partial, beside, below, above, active,
+    outer, inner, partial, beside, below_early, above_early, below_late, above_late, active,
     out, first, second, third, active_here, out_here, in_sem, out_sems
 ):
     depth_z, depth_y, width_x = partial.shape
@@ -321,28 +340,39 @@
     load = pltpu.make_async_copy(active, active_here, in_sem)
     load.start()
     sixth = 1.0 / 6.0
+    ext = slice(8 * len(LATE), 8 * len(LATE) + 8)
 
     def z_scale(p):
         return has_low_z if p < 3 else (has_high_z if p >= depth_z + 3 else 1.0)
 
     def y_scale(t):
         return has_low_y if t == 0 else (has_high_y if t == tiles - 1 else 1.0)
+
+    def arrived(early, late, plane, t, divergence):
+        if not 0 < t < tiles - 1:
+            return late[plane, ext, :]
+        if t - 1 in LATE:
+            return late[plane, rows_of(LATE, t - 1), :]
+        value = early[plane, rows_of(EARLY, t - 1), :]
+        if t - 1 == 7 and divergence:
+            face = late[plane, ext.start + 2 : ext.start + 3, :]
+            value = value + jnp.where(line == 7, face, 0.0)
+        return value
 
     def fill(p):
         z = p - 3
         for t in range(tiles):
             inside = 0 < t < tiles - 1
-            rows = slice(t * 8 - 8, t * 8) if inside else slice(depth_y, depth_y + 8)
             if z < 0:
-                value = below[p, rows, :]
+                value = arrived(below_early, below_late, p, t, True)
                 if z == -1:
                     value = value + (tile_of(outer, inner, 2, 0, t - 1) if inside else beside[depth_z])
             elif z < depth_z:
-                value = partial[z, rows, :] if inside else beside[z]
+                value = partial[z, t * 8 - 8 : t * 8, :] if inside else beside[z]
                 if z == depth_z - 1:
-                    value = value + above[2, rows, :]
+                    value = value + arrived(above_early, above_late, 2, t, False)
             else:
-                value = above[z - depth_z, rows, :]
+                value = arrived(above_early, above_late, z - depth_z, t, True)
             first[p, t * 8 : t * 8 + 8, :] = value * (-sixth * z_scale(p) * y_scale(t))
 
     def around(source, p, t):
@@ -392,7 +422,7 @@
         store.wait()
 
 
-def correct(outer, inner, partial, beside, below, above, active):
+def correct(outer, inner, partial, beside, arrivals, active):
     depth_z, depth_y, width_x = partial.shape
     extended = pltpu.VMEM((depth_z + 5, depth_y + 16, width_x), F32)
     vmem = pl.BlockSpec(memory_space=pltpu.VMEM)
@@ -400,7 +430,7 @@
     out_dims = (3, depth_z, depth_y, width_x)
     return pl.pallas_call(
         correct_kernel,
-        in_specs=[vmem] * 6 + [hbm],
+        in_specs=[vmem] * 8 + [hbm],
         out_specs=hbm,
         out_shape=jax.ShapeDtypeStruct(out_dims, F32),
         scratch_shapes=[extended] * 3
@@ -412,7 +442,7 @@
         ],
         compiler_params=pltpu.CompilerParams(vmem_limit_bytes=CORRECT_BYTES),
         name="correct",
-    )(outer, inner, partial, beside, below, above, active)
+    )(outer, inner, partial, beside, *arrivals, active)
 
 
 def moved(value, axis, steps):
@@ -429,16 +459,20 @@
     out_box = out_box.reshape(slab_count, BOX_ROWS, 1, LANES)
     box = lax.all_to_all(out_box, "slab", split_axis=0, concat_axis=0, tiled=True)
     box = box.reshape(slab_count * BOX_ROWS, LANES)
-    outer, low_rows, high_rows, *tables = sum_outer(box, coarse_field)
+    outer, low_rows, high_rows, low_early, high_early, *tables = sum_outer(box, coarse_field)
     rows_below = moved(low_rows, "pencil", 1)
     rows_above = moved(high_rows, "pencil", -1)
+    below_early = moved(low_early, "slab", 1)
+    above_early = moved(high_early, "slab", -1)
     inner = sum_inner(tables, coarse_field)
-    partial, beside, low_planes, high_planes = diverge(
-        outer, inner, high_rows, rows_below, rows_above
+    early = (below_early, above_early)
+    partial, beside, low_late, high_late = diverge(
+        outer, inner, high_rows, rows_below, rows_above, early
     )
-    below = moved(low_planes, "slab", 1)
-    above = moved(high_planes, "slab", -1)
-    return correct(outer, inner, partial, beside, below, above, active)
+    below_late = moved(low_late, "slab", 1)
+    above_late = moved(high_late, "slab", -1)
+    arrivals = (*early, below_late, above_late)
+    return correct(outer, inner, partial, beside, arrivals, active)
 
 
 def solution(mesh):

time: 144 us -> 148 us (1.028)
  starting transfers between devices: 18 us -> 28.3 us
  waiting for transfers between devices: 18.5 us -> 12.2 us
    ppermute x4 -> x6, starting transfers between devices: 18 us -> 28.3 us  [moved(): return lax.ppermute(value, axis, pairs)]
    ppermute x4 -> x6, waiting for transfers between devices: 18.5 us -> 12.2 us  [moved(): return lax.ppermute(value, axis, pairs)]
    pallas_call x1 -> x2, Pallas kernels: 3.89 us -> 4.47 us  [the longest x1 3.89 us: correct(): pl.pallas_call(correct_kernel, in_specs=[vmem] * 8 + [hbm], out_specs=hbm...]
    pallas_call x3 -> x2, Pallas kernels: 7.91 us -> 7.33 us  [vmem_call(): pl.pallas_call(kernel, in_specs=[vmem] * len(operands), out_specs=[vmem]...]
  transfers between devices with their start and end apart: 4 -> 6, of which waited for: 3 -> 3; matrix products, arithmetic and copies ran while one was open for 0% -> 0% of each run, Pallas kernels for 2% -> 2%
where the time goes in v1:
time: 148 us
  blocking collectives  86.9 us (59%)
  starting transfers between devices  28.3 us (19%)
  Pallas kernels  19.5 us (13%)
  waiting for transfers between devices  12.2 us (8%)
    all_to_all x1, blocking collectives, shards(): lax.all_to_all(out_box, 'slab', split_axis=0, concat_axis=0, tiled=True)  86.9 us
    ppermute x6, starting transfers between devices, moved(): return lax.ppermute(value, axis, pairs)  28.3 us
    ppermute x6, waiting for transfers between devices, moved(): return lax.ppermute(value, axis, pairs)  12.2 us
    pallas_call x1, Pallas kernels, pack(): pl.pallas_call(pack_kernel, in_specs=[pl.BlockSpec(memory_space=pltpu.SME...  7.68 us
    pallas_call x2, Pallas kernels, vmem_call(): pl.pallas_call(kernel, in_specs=[vmem] * len(operands), out_specs=[vmem]...  7.33 us
    pallas_call x1, Pallas kernels, correct(): pl.pallas_call(correct_kernel, in_specs=[vmem] * 8 + [hbm], out_specs=hbm...  3.89 us
  transfers between devices with their start and end apart: 6, of which 3 were waited for; matrix products, arithmetic and copies ran while one was open for 0% of the time, Pallas kernels for 2%

profile of v1, /device:TPU:3, one launch (start us, length us, event | category | flops | bytes accessed | tf_op | source)
XLA Modules:
  0.0 147.8 jit_solution(16824348819225512132)
XLA Ops:
  0.7 7.7 %pack.1 = f32[6208,128]{1,0:T(8,128)} custom-call(s32[1,1]{1,0:T(1,128)S(6)} %copy.8.valid_counts, s32[1,1024]{1,0:T(1,128)} %bitcast.9, s32[1,1024]{1,0:T(1,128)} %row.1, f32[3,1024,256]{2,1,0:T(8,128)} %bitcast.8), custom_call_target="tpu_custom_call" | custom-call | tf_op jit(solution)/shard_map/pack/pallas_call | solution.py:114
  8.3 0.0 copy-start
  8.4 86.9 %all_to_all.5 = f32[64,97,1,128]{3,2,1,0:T(1,128)S(1)} all-to-all(f32[64,97,1,128]{3,2,1,0:T(1,128)} %bitcast.7), channel_id=1, replica_groups=mesh['slab'=64,'pencil'=4] {'slab'}, dimensions={0} | all-to-all | bytes 6356992 | tf_op jit(solution)/shard_map/all_to_all | solution.py:460
  95.2 0.0 copy-done
  95.2 3.9 %sum_outer.1 = (f32[3,4,32,1024]{3,2,1,0:T(8,128)S(1)}, f32[16,1024]{1,0:T(8,128)S(1)}, f32[16,1024]{1,0:T(8,128)S(1)}, f32[3,24,1024]{2,1,0:T(8,128)S(1)}, f32[...) custom-call(f32[6208,128]{1,0:T(8,128)S(1)} %bitcast.6, ...), custom_call_target="tpu_custom_call" | custom-call | tf_op jit(solution)/shard_map/sum_outer/pallas_call | solution.py:246
  99.1 3.7 %collective-permute-start.2 = (f32[3,24,1024]{2,1,0:T(8,128)S(1)}, f32[3,24,1024]{2,1,0:T(8,128)S(1)}, u32[]{:S(2)}, u32[]{:S(2)}) collective-permute-start(f32[3,24,1024]{2,1,0:T(8,128)S(1)} %get-tuple-element.25), channel_id=1, source_target_pairs={{0,4},{4,8},{8,12},{12,16},{16,20},{20,24},{24,28},{28,32},{32,36}... | collective-permute-start | bytes 884744 | tf_op jit(solution)/shard_map/ppermute | solution.py:451
  102.9 6.1 %collective-permute-start.3 = (f32[3,24,1024]{2,1,0:T(8,128)S(1)}, f32[3,24,1024]{2,1,0:T(8,128)S(1)}, u32[]{:S(2)}, u32[]{:S(2)}) collective-permute-start(f32[3,24,1024]{2,1,0:T(8,128)S(1)} %get-tuple-element.26), channel_id=1, source_target_pairs={{4,0},{8,4},{12,8},{16,12},{20,16},{24,20},{28,24},{32,28},{36,32}... | collective-permute-start | bytes 884744 | tf_op jit(solution)/shard_map/ppermute | solution.py:451
  109.0 6.7 %collective-permute-start = (f32[16,1024]{1,0:T(8,128)S(1)}, f32[16,1024]{1,0:T(8,128)S(1)}, u32[]{:S(2)}, u32[]{:S(2)}) collective-permute-start(f32[16,1024]{1,0:T(8,128)S(1)} %get-tuple-element.24), channel_id=1, source_target_pairs={{0,1},{1,2},{2,3},{4,5},{5,6},{6,7},{8,9},{9,10},{10,11},{12,13},{... | collective-permute-start | bytes 196616 | tf_op jit(solution)/shard_map/ppermute | solution.py:451
  115.6 1.9 %collective-permute-start.1 = (f32[16,1024]{1,0:T(8,128)S(1)}, f32[16,1024]{1,0:T(8,128)S(1)}, u32[]{:S(2)}, u32[]{:S(2)}) collective-permute-start(f32[16,1024]{1,0:T(8,128)S(1)} %get-tuple-element.23.own), channel_id=1, source_target_pairs={{1,0},{2,1},{3,2},{5,4},{6,5},{7,6},{9,8},{10,9},{11,10},{13,12},{... | collective-permute-start | bytes 196616 | tf_op jit(solution)/shard_map/ppermute | solution.py:451
  117.5 3.4 %sum_inner.1.inner = f32[3,4,32,1024]{3,2,1,0:T(8,128)S(1)} custom-call(bf16[2048,768]{1,0:T(8,128)(2,1)S(1)} %get-tuple-element.19.rows16, bf16[64,2048]{1,0:T(8,128)(2,1)S(1)} %get-tuple-element.20.line_hot, bf16[32,2048]{1,0:T(8,128)(2,1)S(1)} %get-tuple-element.21.tile_hot, f32[32,64,128]{2,1,0:T(8,128)S(1)} %get-tuple-element.22.number, ...), custom_call_target="tpu_custom_call" | custom-call | tf_op jit(solution)/shard_map/sum_inner/pallas_call | solution.py:246
  121.0 0.0 copy-start.1
  121.0 0.0 collective-permute-done.below
  121.0 0.2 collective-permute-done.1.above
  121.2 0.0 collective-permute-done.2.below_early
  121.2 0.0 collective-permute-done.3.above_early
  121.2 0.6 diverge.1
  121.8 1.9 %collective-permute-start.4 = (f32[3,48,1024]{2,1,0:T(8,128)S(1)}, f32[3,48,1024]{2,1,0:T(8,128)S(1)}, u32[]{:S(2)}, u32[]{:S(2)}) collective-permute-start(f32[3,48,1024]{2,1,0:T(8,128)S(1)} %get-tuple-element.29), channel_id=1, source_target_pairs={{0,4},{4,8},{8,12},{12,16},{16,20},{20,24},{24,28},{28,32},{32,36}... | collective-permute-start | bytes 1769480 | tf_op jit(solution)/shard_map/ppermute | solution.py:451
  123.7 8.1 %collective-permute-start.5 = (f32[3,48,1024]{2,1,0:T(8,128)S(1)}, f32[3,48,1024]{2,1,0:T(8,128)S(1)}, u32[]{:S(2)}, u32[]{:S(2)}) collective-permute-start(f32[3,48,1024]{2,1,0:T(8,128)S(1)} %get-tuple-element.30), channel_id=1, source_target_pairs={{4,0},{8,4},{12,8},{16,12},{20,16},{24,20},{28,24},{32,28},{36,32}... | collective-permute-start | bytes 1769480 | tf_op jit(solution)/shard_map/ppermute | solution.py:451
  131.8 10.2 %collective-permute-done.4.below_late = f32[3,48,1024]{2,1,0:T(8,128)S(1)} collective-permute-done((f32[3,48,1024]{2,1,0:T(8,128)S(1)}, f32[3,48,1024]{2,1,0:T(8,128)S(1)}, u32[]{:S(2)}, u32[]{:S(2)}) %collective-permute-start.4) | collective-permute-done | bytes 589856 | tf_op jit(solution)/shard_map/ppermute | solution.py:451
  142.0 1.8 %collective-permute-done.5.above_late = f32[3,48,1024]{2,1,0:T(8,128)S(1)} collective-permute-done((f32[3,48,1024]{2,1,0:T(8,128)S(1)}, f32[3,48,1024]{2,1,0:T(8,128)S(1)}, u32[]{:S(2)}, u32[]{:S(2)}) %collective-permute-start.5) | collective-permute-done | bytes 589856 | tf_op jit(solution)/shard_map/ppermute | solution.py:451
  143.8 0.0 copy-done.1
  143.8 3.9 %correct.1 = f32[3,4,64,1024]{3,2,1,0:T(8,128)} custom-call(f32[3,4,32,1024]{3,2,1,0:T(8,128)S(1)} %get-tuple-element.18.outer, f32[3,4,32,1024]{3,2,1,0:T(8,128)S(1)} %sum_inner.1.inner, f32[4,64,1024]{2,1,0:T(8,128)S(1)} %get-tuple-element.27.partial, f32[5,8,1024]{2,1,0:T(8,128)S(1)} %get-tuple-element.28.beside, ...), custom_call_target="tpu_custom_call" | custom-call | tf_op jit(solution)/shard_map/correct/pallas_call | solution.py:431
Async XLA Ops:
  8.3 86.9 %copy-start = (f32[3,4,64,1024]{3,2,1,0:T(8,128)S(1)}, f32[3,4,64,1024]{3,2,1,0:T(8,128)}, u32[]{:S(2)}) copy-start(f32[3,4,64,1024]{3,2,1,0:T(8,128)} %base.3) | copy-start | bytes 9437188
  99.1 22.1 %collective-permute-start.2 = (f32[3,24,1024]{2,1,0:T(8,128)S(1)}, f32[3,24,1024]{2,1,0:T(8,128)S(1)}, u32[]{:S(2)}, u32[]{:S(2)}) collective-permute-start(f32[3,24,1024]{2,1,0:T(8,128)S(1)} %get-tuple-element.25), channel_id=1, source_target_pairs={{0,4},{4,8},{8,12},{12,16},{16,20},{20,24},{24,28},{28,32},{32,36}... | collective-permute-start | bytes 884744 | tf_op jit(solution)/shard_map/ppermute | solution.py:451
  102.9 18.3 %collective-permute-start.3 = (f32[3,24,1024]{2,1,0:T(8,128)S(1)}, f32[3,24,1024]{2,1,0:T(8,128)S(1)}, u32[]{:S(2)}, u32[]{:S(2)}) collective-permute-start(f32[3,24,1024]{2,1,0:T(8,128)S(1)} %get-tuple-element.26), channel_id=1, source_target_pairs={{4,0},{8,4},{12,8},{16,12},{20,16},{24,20},{28,24},{32,28},{36,32}... | collective-permute-start | bytes 884744 | tf_op jit(solution)/shard_map/ppermute | solution.py:451
  109.0 12.0 %collective-permute-start = (f32[16,1024]{1,0:T(8,128)S(1)}, f32[16,1024]{1,0:T(8,128)S(1)}, u32[]{:S(2)}, u32[]{:S(2)}) collective-permute-start(f32[16,1024]{1,0:T(8,128)S(1)} %get-tuple-element.24), channel_id=1, source_target_pairs={{0,1},{1,2},{2,3},{4,5},{5,6},{6,7},{8,9},{9,10},{10,11},{12,13},{... | collective-permute-start | bytes 196616 | tf_op jit(solution)/shard_map/ppermute | solution.py:451
  115.6 5.6 %collective-permute-start.1 = (f32[16,1024]{1,0:T(8,128)S(1)}, f32[16,1024]{1,0:T(8,128)S(1)}, u32[]{:S(2)}, u32[]{:S(2)}) collective-permute-start(f32[16,1024]{1,0:T(8,128)S(1)} %get-tuple-element.23.own), channel_id=1, source_target_pairs={{1,0},{2,1},{3,2},{5,4},{6,5},{7,6},{9,8},{10,9},{11,10},{13,12},{... | collective-permute-start | bytes 196616 | tf_op jit(solution)/shard_map/ppermute | solution.py:451
  121.0 22.8 %copy-start.1 = (s32[4,64,1024]{2,1,0:T(8,128)S(1)}, s32[4,64,1024]{2,1,0:T(8,128)}, u32[]{:S(2)}) copy-start(s32[4,64,1024]{2,1,0:T(8,128)} %active.1) | copy-start | bytes 3145732
  121.8 20.2 %collective-permute-start.4 = (f32[3,48,1024]{2,1,0:T(8,128)S(1)}, f32[3,48,1024]{2,1,0:T(8,128)S(1)}, u32[]{:S(2)}, u32[]{:S(2)}) collective-permute-start(f32[3,48,1024]{2,1,0:T(8,128)S(1)} %get-tuple-element.29), channel_id=1, source_target_pairs={{0,4},{4,8},{8,12},{12,16},{16,20},{20,24},{24,28},{28,32},{32,36}... | collective-permute-start | bytes 1769480 | tf_op jit(solution)/shard_map/ppermute | solution.py:451
  123.7 20.0 %collective-permute-start.5 = (f32[3,48,1024]{2,1,0:T(8,128)S(1)}, f32[3,48,1024]{2,1,0:T(8,128)S(1)}, u32[]{:S(2)}, u32[]{:S(2)}) collective-permute-start(f32[3,48,1024]{2,1,0:T(8,128)S(1)} %get-tuple-element.30), channel_id=1, source_target_pairs={{4,0},{8,4},{12,8},{16,12},{20,16},{24,20},{28,24},{32,28},{36,32}... | collective-permute-start | bytes 1769480 | tf_op jit(solution)/shard_map/ppermute | solution.py:451

commit v2 on v0

--- a/solution.py
+++ b/solution.py
@@ -74,6 +74,7 @@
         table = table + dot_rows(upper, place) * 64.0 + dot_rows(lower, place)
     rank16 = jnp.concatenate(rank_all, axis=1)
     named16 = jnp.concatenate([named.astype(BF16) for named in named_all], axis=1)
+    loads[0].wait()
     for g in range(slab_count):
         chosen[g * SLOTS : (g + 1) * SLOTS, :] = rank16 * named16[g : g + 1, :]
         start = g * BOX_ROWS + TAG_ROW
@@ -84,7 +85,8 @@
     chunk = min(256, count_held)
     stores = []
     for part in range(3):
-        loads[part].wait()
+        if part > 0:
+            loads[part].wait()
         for start in range(0, count_held, chunk):
             rows = slice(start, start + chunk)
             high, low = halves(arrived[part, rows, :])
@@ -154,11 +156,13 @@
     return (next_x - face_x) + (next_y - face_y) + (above_z - face_z)
 
 
-def put_plane(low_planes, high_planes, depth_z, z, rows, value):
+def put_plane(low_planes, high_planes, depth_z, z, tile, value):
     if z > depth_z - 4:
-        low_planes[z - depth_z + 3, rows, :] = value
+        start = (z - depth_z + 3) * 64 + tile * 8
+        low_planes[start : start + 8, :] = value
     if z < 2:
-        high_planes[z, rows, :] = value
+        start = z * 64 + tile * 8
+        high_planes[start : start + 8, :] = value
 
 
 def sum_tiles(tiles, rows16, line_hot, tile_hot, number, base, field):
@@ -277,10 +281,9 @@
                 value = value + jnp.where(iota(value.shape, 0) == 7, face, 0.0)
             rows = slice(tile * 8, tile * 8 + 8)
             partial[z, rows, :] = value
-            put_plane(low_planes, high_planes, depth_z, z, rows, value)
+            put_plane(low_planes, high_planes, depth_z, z, tile, value)
             if z == 0:
-                high_planes[2, rows, :] = tile_of(outer, inner, 2, 0, tile)
-    ext = slice(64, 72)
+                high_planes[128 + tile * 8 : 136 + tile * 8, :] = tile_of(outer, inner, 2, 0, tile)
     for z in range(depth_z + 1):
         beside[z, 0:3, :] = above[3 * z : 3 * z + 3, :]
         beside[z, 3:5, :] = jnp.zeros_like(beside[z, 3:5, :])
@@ -289,16 +292,18 @@
             face = own[3 * z + 2 : 3 * z + 3, :]
             under = under + jnp.where(iota(under.shape, 0) == 2, face, 0.0)
         beside[z, 5:8, :] = under
-        if z < depth_z:
-            put_plane(low_planes, high_planes, depth_z, z, ext, beside[z])
-        else:
-            high_planes[2, ext, :] = beside[z]
+    low_planes[192:200, :] = beside[depth_z - 1]
+    low_planes[194:195, :] = beside[depth_z - 2, 0:1, :]
+    low_planes[197:198, :] = beside[depth_z - 2, 7:8, :]
+    high_planes[192:200, :] = beside[0]
+    high_planes[197:198, :] = beside[1, 7:8, :]
+    high_planes[200:208, :] = beside[depth_z]
 
 
 def diverge(outer, inner, own, below, above):
     depth_z, width_x = outer.shape[1], outer.shape[3]
     shapes = [((depth_z, 64, width_x), F32), ((depth_z + 1, 8, width_x), F32)]
-    shapes += [((3, 72, width_x), F32)] * 2
+    shapes += [((200, width_x), F32), ((208, width_x), F32)]
     return vmem_call(diverge_kernel, shapes, DIVERGE_BYTES, "diverge")(
         outer, inner, own, below, above
     )
@@ -328,21 +333,29 @@
     def y_scale(t):
         return has_low_y if t == 0 else (has_high_y if t == tiles - 1 else 1.0)
 
+    def halo_tile(planes, plane, t, away):
+        if 0 < t < tiles - 1:
+            return planes[plane * 64 + t * 8 - 8 : plane * 64 + t * 8, :]
+        if away > 1:
+            return jnp.zeros((8, width_x), F32)
+        value = planes[192:200, :]
+        return value if away == 0 else pltpu.roll(value, 2 if t == 0 else 6, 0)
+
     def fill(p):
         z = p - 3
         for t in range(tiles):
             inside = 0 < t < tiles - 1
-            rows = slice(t * 8 - 8, t * 8) if inside else slice(depth_y, depth_y + 8)
+            rows = slice(t * 8 - 8, t * 8)
             if z < 0:
-                value = below[p, rows, :]
+                value = halo_tile(below, p, t, 2 - p)
                 if z == -1:
                     value = value + (tile_of(outer, inner, 2, 0, t - 1) if inside else beside[depth_z])
             elif z < depth_z:
                 value = partial[z, rows, :] if inside else beside[z]
                 if z == depth_z - 1:
-                    value = value + above[2, rows, :]
+                    value = value + (halo_tile(above, 2, t, 0) if inside else above[200:208, :])
             else:
-                value = above[z - depth_z, rows, :]
+                value = halo_tile(above, z - depth_z, t, z - depth_z)
             first[p, t * 8 : t * 8 + 8, :] = value * (-sixth * z_scale(p) * y_scale(t))
 
     def around(source, p, t):

time: 144 us -> 146 us (1.014)
  waiting for transfers between devices: 18.5 us -> 22.9 us
  starting transfers between devices: 18 us -> 15.8 us
    ppermute x4, waiting for transfers between devices: 18.5 us -> 22.9 us  [moved(): return lax.ppermute(value, axis, pairs)]
    ppermute x4, starting transfers between devices: 18 us -> 15.8 us  [moved(): return lax.ppermute(value, axis, pairs)]
  transfers between devices with their start and end apart: 4 -> 4, of which waited for: 3 -> 2; matrix products, arithmetic and copies ran while one was open for 0% -> 0% of each run, Pallas kernels for 2% -> 2%
where the time goes in v2:
time: 146 us
  blocking collectives  86.9 us (60%)
  waiting for transfers between devices  22.9 us (16%)
  Pallas kernels  19.5 us (13%)
  starting transfers between devices  15.8 us (11%)
    all_to_all x1, blocking collectives, shards(): lax.all_to_all(out_box, 'slab', split_axis=0, concat_axis=0, tiled=True)  86.9 us
    ppermute x4, waiting for transfers between devices, moved(): return lax.ppermute(value, axis, pairs)  22.9 us
    ppermute x4, starting transfers between devices, moved(): return lax.ppermute(value, axis, pairs)  15.8 us
    pallas_call x3, Pallas kernels, vmem_call(): pl.pallas_call(kernel, in_specs=[vmem] * len(operands), out_specs=[vmem]...  7.9 us
    pallas_call x1, Pallas kernels, pack(): pl.pallas_call(pack_kernel, in_specs=[pl.BlockSpec(memory_space=pltpu.SME...  7.68 us
    pallas_call x1, Pallas kernels, correct(): pl.pallas_call(correct_kernel, in_specs=[vmem] * 6 + [hbm], out_specs=hbm...  3.9 us
  transfers between devices with their start and end apart: 4, of which 2 were waited for; matrix products, arithmetic and copies ran while one was open for 0% of the time, Pallas kernels for 2%

profile of v2, /device:TPU:3, one launch (start us, length us, event | category | flops | bytes accessed | tf_op | source)
XLA Modules:
  0.0 146.0 jit_solution(7242788362710811252)
XLA Ops:
  0.7 7.7 %pack.1 = f32[6208,128]{1,0:T(8,128)} custom-call(s32[1,1]{1,0:T(1,128)S(6)} %copy.8.valid_counts, s32[1,1024]{1,0:T(1,128)} %bitcast.9, s32[1,1024]{1,0:T(1,128)} %row.1, f32[3,1024,256]{2,1,0:T(8,128)} %bitcast.8), custom_call_target="tpu_custom_call" | custom-call | tf_op jit(solution)/shard_map/pack/pallas_call | solution.py:116
  8.3 0.0 copy-start
  8.3 86.9 %all_to_all.5 = f32[64,97,1,128]{3,2,1,0:T(1,128)S(1)} all-to-all(f32[64,97,1,128]{3,2,1,0:T(1,128)} %bitcast.7), channel_id=1, replica_groups=mesh['slab'=64,'pencil'=4] {'slab'}, dimensions={0} | all-to-all | bytes 6356992 | tf_op jit(solution)/shard_map/all_to_all | solution.py:443
  95.2 0.0 copy-done
  95.2 3.9 %sum_outer.1 = (f32[3,4,32,1024]{3,2,1,0:T(8,128)S(1)}, f32[16,1024]{1,0:T(8,128)S(1)}, f32[16,1024]{1,0:T(8,128)S(1)}, bf16[2048,768]{1,0:T(8,128)(2,1)S(1)}, b...) custom-call(f32[6208,128]{1,0:T(8,128)S(1)} %bitcast.6, ...), custom_call_target="tpu_custom_call" | custom-call | tf_op jit(solution)/shard_map/sum_outer/pallas_call | solution.py:242
  99.1 6.1 %collective-permute-start = (f32[16,1024]{1,0:T(8,128)S(1)}, f32[16,1024]{1,0:T(8,128)S(1)}, u32[]{:S(2)}, u32[]{:S(2)}) collective-permute-start(f32[16,1024]{1,0:T(8,128)S(1)} %get-tuple-element.22), channel_id=1, source_target_pairs={{0,1},{1,2},{2,3},{4,5},{5,6},{6,7},{8,9},{9,10},{10,11},{12,13},{... | collective-permute-start | bytes 196616 | tf_op jit(solution)/shard_map/ppermute | solution.py:434
  105.2 1.9 %collective-permute-start.1 = (f32[16,1024]{1,0:T(8,128)S(1)}, f32[16,1024]{1,0:T(8,128)S(1)}, u32[]{:S(2)}, u32[]{:S(2)}) collective-permute-start(f32[16,1024]{1,0:T(8,128)S(1)} %get-tuple-element.21.own), channel_id=1, source_target_pairs={{1,0},{2,1},{3,2},{5,4},{6,5},{7,6},{9,8},{10,9},{11,10},{13,12},{... | collective-permute-start | bytes 196616 | tf_op jit(solution)/shard_map/ppermute | solution.py:434
  107.1 3.4 %sum_inner.1.inner = f32[3,4,32,1024]{3,2,1,0:T(8,128)S(1)} custom-call(bf16[2048,768]{1,0:T(8,128)(2,1)S(1)} %get-tuple-element.17.rows16, bf16[64,2048]{1,0:T(8,128)(2,1)S(1)} %get-tuple-element.18.line_hot, bf16[32,2048]{1,0:T(8,128)(2,1)S(1)} %get-tuple-element.19.tile_hot, f32[32,64,128]{2,1,0:T(8,128)S(1)} %get-tuple-element.20.number, ...), custom_call_target="tpu_custom_call" | custom-call | tf_op jit(solution)/shard_map/sum_inner/pallas_call | solution.py:242
  110.5 0.0 copy-start.1
  110.6 0.0 collective-permute-done.below
  110.6 0.2 collective-permute-done.1.above
  110.8 0.6 diverge.1
  111.4 5.7 %collective-permute-start.3 = (f32[208,1024]{1,0:T(8,128)S(1)}, f32[208,1024]{1,0:T(8,128)S(1)}, u32[]{:S(2)}, u32[]{:S(2)}) collective-permute-start(f32[208,1024]{1,0:T(8,128)S(1)} %get-tuple-element.26), channel_id=1, source_target_pairs={{4,0},{8,4},{12,8},{16,12},{20,16},{24,20},{28,24},{32,28},{36,32}... | collective-permute-start | bytes 2555912 | tf_op jit(solution)/shard_map/ppermute | solution.py:434
  117.1 2.1 %collective-permute-start.2 = (f32[200,1024]{1,0:T(8,128)S(1)}, f32[200,1024]{1,0:T(8,128)S(1)}, u32[]{:S(2)}, u32[]{:S(2)}) collective-permute-start(f32[200,1024]{1,0:T(8,128)S(1)} %get-tuple-element.25), channel_id=1, source_target_pairs={{0,4},{4,8},{8,12},{12,16},{16,20},{20,24},{24,28},{28,32},{32,36}... | collective-permute-start | bytes 2457608 | tf_op jit(solution)/shard_map/ppermute | solution.py:434
  119.2 22.7 %collective-permute-done.2.below = f32[200,1024]{1,0:T(8,128)S(1)} collective-permute-done((f32[200,1024]{1,0:T(8,128)S(1)}, f32[200,1024]{1,0:T(8,128)S(1)}, u32[]{:S(2)}, u32[]{:S(2)}) %collective-permute-start.2) | collective-permute-done | bytes 819232 | tf_op jit(solution)/shard_map/ppermute | solution.py:434
  141.9 0.0 collective-permute-done.3.above
  141.9 0.0 copy-done.1
  141.9 3.9 %correct.1 = f32[3,4,64,1024]{3,2,1,0:T(8,128)} custom-call(f32[3,4,32,1024]{3,2,1,0:T(8,128)S(1)} %get-tuple-element.16.outer, f32[3,4,32,1024]{3,2,1,0:T(8,128)S(1)} %sum_inner.1.inner, f32[4,64,1024]{2,1,0:T(8,128)S(1)} %get-tuple-element.23.partial, f32[5,8,1024]{2,1,0:T(8,128)S(1)} %get-tuple-element.24.beside, ...), custom_call_target="tpu_custom_call" | custom-call | tf_op jit(solution)/shard_map/correct/pallas_call | solution.py:414
Async XLA Ops:
  8.3 86.9 %copy-start = (f32[3,4,64,1024]{3,2,1,0:T(8,128)S(1)}, f32[3,4,64,1024]{3,2,1,0:T(8,128)}, u32[]{:S(2)}) copy-start(f32[3,4,64,1024]{3,2,1,0:T(8,128)} %base.3) | copy-start | bytes 9437188
  99.1 11.5 %collective-permute-start = (f32[16,1024]{1,0:T(8,128)S(1)}, f32[16,1024]{1,0:T(8,128)S(1)}, u32[]{:S(2)}, u32[]{:S(2)}) collective-permute-start(f32[16,1024]{1,0:T(8,128)S(1)} %get-tuple-element.22), channel_id=1, source_target_pairs={{0,1},{1,2},{2,3},{4,5},{5,6},{6,7},{8,9},{9,10},{10,11},{12,13},{... | collective-permute-start | bytes 196616 | tf_op jit(solution)/shard_map/ppermute | solution.py:434
  105.2 5.6 %collective-permute-start.1 = (f32[16,1024]{1,0:T(8,128)S(1)}, f32[16,1024]{1,0:T(8,128)S(1)}, u32[]{:S(2)}, u32[]{:S(2)}) collective-permute-start(f32[16,1024]{1,0:T(8,128)S(1)} %get-tuple-element.21.own), channel_id=1, source_target_pairs={{1,0},{2,1},{3,2},{5,4},{6,5},{7,6},{9,8},{10,9},{11,10},{13,12},{... | collective-permute-start | bytes 196616 | tf_op jit(solution)/shard_map/ppermute | solution.py:434
  110.5 31.4 %copy-start.1 = (s32[4,64,1024]{2,1,0:T(8,128)S(1)}, s32[4,64,1024]{2,1,0:T(8,128)}, u32[]{:S(2)}) copy-start(s32[4,64,1024]{2,1,0:T(8,128)} %active.1) | copy-start | bytes 3145732
  111.4 30.5 %collective-permute-start.3 = (f32[208,1024]{1,0:T(8,128)S(1)}, f32[208,1024]{1,0:T(8,128)S(1)}, u32[]{:S(2)}, u32[]{:S(2)}) collective-permute-start(f32[208,1024]{1,0:T(8,128)S(1)} %get-tuple-element.26), channel_id=1, source_target_pairs={{4,0},{8,4},{12,8},{16,12},{20,16},{24,20},{28,24},{32,28},{36,32}... | collective-permute-start | bytes 2555912 | tf_op jit(solution)/shard_map/ppermute | solution.py:434
  117.1 24.8 %collective-permute-start.2 = (f32[200,1024]{1,0:T(8,128)S(1)}, f32[200,1024]{1,0:T(8,128)S(1)}, u32[]{:S(2)}, u32[]{:S(2)}) collective-permute-start(f32[200,1024]{1,0:T(8,128)S(1)} %get-tuple-element.25), channel_id=1, source_target_pairs={{0,4},{4,8},{8,12},{12,16},{16,20},{20,24},{24,28},{28,32},{32,36}... | collective-permute-start | bytes 2457608 | tf_op jit(solution)/shard_map/ppermute | solution.py:434

commit v3 on v2

--- a/solution.py
+++ b/solution.py
@@ -293,6 +293,7 @@
             under = under + jnp.where(iota(under.shape, 0) == 2, face, 0.0)
         beside[z, 5:8, :] = under
     low_planes[192:200, :] = beside[depth_z - 1]
+    low_planes[200:208, :] = jnp.zeros_like(low_planes[200:208, :])
     low_planes[194:195, :] = beside[depth_z - 2, 0:1, :]
     low_planes[197:198, :] = beside[depth_z - 2, 7:8, :]
     high_planes[192:200, :] = beside[0]
@@ -303,7 +304,7 @@
 def diverge(outer, inner, own, below, above):
     depth_z, width_x = outer.shape[1], outer.shape[3]
     shapes = [((depth_z, 64, width_x), F32), ((depth_z + 1, 8, width_x), F32)]
-    shapes += [((200, width_x), F32), ((208, width_x), F32)]
+    shapes += [((208, width_x), F32)] * 2
     return vmem_call(diverge_kernel, shapes, DIVERGE_BYTES, "diverge")(
         outer, inner, own, below, above
     )

time: 146 us -> 143 us (0.979)
  waiting for transfers between devices: 22.9 us -> 17.8 us
  starting transfers between devices: 15.8 us -> 18 us
    ppermute x4, waiting for transfers between devices: 22.9 us -> 17.8 us  [moved(): return lax.ppermute(value, axis, pairs)]
    ppermute x4, starting transfers between devices: 15.8 us -> 18 us  [moved(): return lax.ppermute(value, axis, pairs)]
  transfers between devices with their start and end apart: 4 -> 4, of which waited for: 2 -> 3; matrix products, arithmetic and copies ran while one was open for 0% -> 0% of each run, Pallas kernels for 2% -> 2%
where the time goes in v3:
time: 143 us
  blocking collectives  86.9 us (61%)
  Pallas kernels  19.5 us (14%)
  starting transfers between devices  18 us (13%)
  waiting for transfers between devices  17.8 us (12%)
    all_to_all x1, blocking collectives, shards(): lax.all_to_all(out_box, 'slab', split_axis=0, concat_axis=0, tiled=True)  86.9 us
    ppermute x4, starting transfers between devices, moved(): return lax.ppermute(value, axis, pairs)  18 us
    ppermute x4, waiting for transfers between devices, moved(): return lax.ppermute(value, axis, pairs)  17.8 us
    pallas_call x3, Pallas kernels, vmem_call(): pl.pallas_call(kernel, in_specs=[vmem] * len(operands), out_specs=[vmem]...  7.9 us
    pallas_call x1, Pallas kernels, pack(): pl.pallas_call(pack_kernel, in_specs=[pl.BlockSpec(memory_space=pltpu.SME...  7.68 us
    pallas_call x1, Pallas kernels, correct(): pl.pallas_call(correct_kernel, in_specs=[vmem] * 6 + [hbm], out_specs=hbm...  3.89 us
  transfers between devices with their start and end apart: 4, of which 3 were waited for; matrix products, arithmetic and copies ran while one was open for 0% of the time, Pallas kernels for 2%

profile of v3, /device:TPU:3, one launch (start us, length us, event | category | flops | bytes accessed | tf_op | source)
XLA Modules:
  0.0 143.0 jit_solution(15047873358747376167)
XLA Ops:
  0.7 7.7 %pack.1 = f32[6208,128]{1,0:T(8,128)} custom-call(s32[1,1]{1,0:T(1,128)S(6)} %copy.8.valid_counts, s32[1,1024]{1,0:T(1,128)} %bitcast.9, s32[1,1024]{1,0:T(1,128)} %row.1, f32[3,1024,256]{2,1,0:T(8,128)} %bitcast.8), custom_call_target="tpu_custom_call" | custom-call | tf_op jit(solution)/shard_map/pack/pallas_call | solution.py:116
  8.3 0.0 copy-start
  8.3 86.9 %all_to_all.5 = f32[64,97,1,128]{3,2,1,0:T(1,128)S(1)} all-to-all(f32[64,97,1,128]{3,2,1,0:T(1,128)} %bitcast.7), channel_id=1, replica_groups=mesh['slab'=64,'pencil'=4] {'slab'}, dimensions={0} | all-to-all | bytes 6356992 | tf_op jit(solution)/shard_map/all_to_all | solution.py:444
  95.2 0.0 copy-done
  95.2 3.9 %sum_outer.1 = (f32[3,4,32,1024]{3,2,1,0:T(8,128)S(1)}, f32[16,1024]{1,0:T(8,128)S(1)}, f32[16,1024]{1,0:T(8,128)S(1)}, bf16[2048,768]{1,0:T(8,128)(2,1)S(1)}, b...) custom-call(f32[6208,128]{1,0:T(8,128)S(1)} %bitcast.6, ...), custom_call_target="tpu_custom_call" | custom-call | tf_op jit(solution)/shard_map/sum_outer/pallas_call | solution.py:242
  99.1 6.1 %collective-permute-start = (f32[16,1024]{1,0:T(8,128)S(1)}, f32[16,1024]{1,0:T(8,128)S(1)}, u32[]{:S(2)}, u32[]{:S(2)}) collective-permute-start(f32[16,1024]{1,0:T(8,128)S(1)} %get-tuple-element.22), channel_id=1, source_target_pairs={{0,1},{1,2},{2,3},{4,5},{5,6},{6,7},{8,9},{9,10},{10,11},{12,13},{... | collective-permute-start | bytes 196616 | tf_op jit(solution)/shard_map/ppermute | solution.py:435
  105.2 1.9 %collective-permute-start.1 = (f32[16,1024]{1,0:T(8,128)S(1)}, f32[16,1024]{1,0:T(8,128)S(1)}, u32[]{:S(2)}, u32[]{:S(2)}) collective-permute-start(f32[16,1024]{1,0:T(8,128)S(1)} %get-tuple-element.21.own), channel_id=1, source_target_pairs={{1,0},{2,1},{3,2},{5,4},{6,5},{7,6},{9,8},{10,9},{11,10},{13,12},{... | collective-permute-start | bytes 196616 | tf_op jit(solution)/shard_map/ppermute | solution.py:435
  107.1 3.4 %sum_inner.1.inner = f32[3,4,32,1024]{3,2,1,0:T(8,128)S(1)} custom-call(bf16[2048,768]{1,0:T(8,128)(2,1)S(1)} %get-tuple-element.17.rows16, bf16[64,2048]{1,0:T(8,128)(2,1)S(1)} %get-tuple-element.18.line_hot, bf16[32,2048]{1,0:T(8,128)(2,1)S(1)} %get-tuple-element.19.tile_hot, f32[32,64,128]{2,1,0:T(8,128)S(1)} %get-tuple-element.20.number, ...), custom_call_target="tpu_custom_call" | custom-call | tf_op jit(solution)/shard_map/sum_inner/pallas_call | solution.py:242
  110.5 0.0 copy-start.1
  110.6 0.0 collective-permute-done.below
  110.6 0.2 collective-permute-done.1.above
  110.8 0.6 diverge.1
  111.4 2.9 %collective-permute-start.2 = (f32[208,1024]{1,0:T(8,128)S(1)}, f32[208,1024]{1,0:T(8,128)S(1)}, u32[]{:S(2)}, u32[]{:S(2)}) collective-permute-start(f32[208,1024]{1,0:T(8,128)S(1)} %get-tuple-element.25), channel_id=1, source_target_pairs={{0,4},{4,8},{8,12},{12,16},{16,20},{20,24},{24,28},{28,32},{32,36}... | collective-permute-start | bytes 2555912 | tf_op jit(solution)/shard_map/ppermute | solution.py:435
  114.3 7.1 %collective-permute-start.3 = (f32[208,1024]{1,0:T(8,128)S(1)}, f32[208,1024]{1,0:T(8,128)S(1)}, u32[]{:S(2)}, u32[]{:S(2)}) collective-permute-start(f32[208,1024]{1,0:T(8,128)S(1)} %get-tuple-element.26), channel_id=1, source_target_pairs={{4,0},{8,4},{12,8},{16,12},{20,16},{24,20},{28,24},{32,28},{36,32}... | collective-permute-start | bytes 2555912 | tf_op jit(solution)/shard_map/ppermute | solution.py:435
  121.4 15.8 %collective-permute-done.2.below = f32[208,1024]{1,0:T(8,128)S(1)} collective-permute-done((f32[208,1024]{1,0:T(8,128)S(1)}, f32[208,1024]{1,0:T(8,128)S(1)}, u32[]{:S(2)}, u32[]{:S(2)}) %collective-permute-start.2) | collective-permute-done | bytes 852000 | tf_op jit(solution)/shard_map/ppermute | solution.py:435
  137.2 1.8 %collective-permute-done.3.above = f32[208,1024]{1,0:T(8,128)S(1)} collective-permute-done((f32[208,1024]{1,0:T(8,128)S(1)}, f32[208,1024]{1,0:T(8,128)S(1)}, u32[]{:S(2)}, u32[]{:S(2)}) %collective-permute-start.3) | collective-permute-done | bytes 852000 | tf_op jit(solution)/shard_map/ppermute | solution.py:435
  139.0 0.0 copy-done.1
  139.0 3.9 %correct.1 = f32[3,4,64,1024]{3,2,1,0:T(8,128)} custom-call(f32[3,4,32,1024]{3,2,1,0:T(8,128)S(1)} %get-tuple-element.16.outer, f32[3,4,32,1024]{3,2,1,0:T(8,128)S(1)} %sum_inner.1.inner, f32[4,64,1024]{2,1,0:T(8,128)S(1)} %get-tuple-element.23.partial, f32[5,8,1024]{2,1,0:T(8,128)S(1)} %get-tuple-element.24.beside, ...), custom_call_target="tpu_custom_call" | custom-call | tf_op jit(solution)/shard_map/correct/pallas_call | solution.py:415
Async XLA Ops:
  8.3 86.9 %copy-start = (f32[3,4,64,1024]{3,2,1,0:T(8,128)S(1)}, f32[3,4,64,1024]{3,2,1,0:T(8,128)}, u32[]{:S(2)}) copy-start(f32[3,4,64,1024]{3,2,1,0:T(8,128)} %base.3) | copy-start | bytes 9437188
  99.1 11.5 %collective-permute-start = (f32[16,1024]{1,0:T(8,128)S(1)}, f32[16,1024]{1,0:T(8,128)S(1)}, u32[]{:S(2)}, u32[]{:S(2)}) collective-permute-start(f32[16,1024]{1,0:T(8,128)S(1)} %get-tuple-element.22), channel_id=1, source_target_pairs={{0,1},{1,2},{2,3},{4,5},{5,6},{6,7},{8,9},{9,10},{10,11},{12,13},{... | collective-permute-start | bytes 196616 | tf_op jit(solution)/shard_map/ppermute | solution.py:435
  105.2 5.6 %collective-permute-start.1 = (f32[16,1024]{1,0:T(8,128)S(1)}, f32[16,1024]{1,0:T(8,128)S(1)}, u32[]{:S(2)}, u32[]{:S(2)}) collective-permute-start(f32[16,1024]{1,0:T(8,128)S(1)} %get-tuple-element.21.own), channel_id=1, source_target_pairs={{1,0},{2,1},{3,2},{5,4},{6,5},{7,6},{9,8},{10,9},{11,10},{13,12},{... | collective-permute-start | bytes 196616 | tf_op jit(solution)/shard_map/ppermute | solution.py:435
  110.5 28.4 %copy-start.1 = (s32[4,64,1024]{2,1,0:T(8,128)S(1)}, s32[4,64,1024]{2,1,0:T(8,128)}, u32[]{:S(2)}) copy-start(s32[4,64,1024]{2,1,0:T(8,128)} %active.1) | copy-start | bytes 3145732
  111.4 25.8 %collective-permute-start.2 = (f32[208,1024]{1,0:T(8,128)S(1)}, f32[208,1024]{1,0:T(8,128)S(1)}, u32[]{:S(2)}, u32[]{:S(2)}) collective-permute-start(f32[208,1024]{1,0:T(8,128)S(1)} %get-tuple-element.25), channel_id=1, source_target_pairs={{0,4},{4,8},{8,12},{12,16},{16,20},{20,24},{24,28},{28,32},{32,36}... | collective-permute-start | bytes 2555912 | tf_op jit(solution)/shard_map/ppermute | solution.py:435
  114.3 24.7 %collective-permute-start.3 = (f32[208,1024]{1,0:T(8,128)S(1)}, f32[208,1024]{1,0:T(8,128)S(1)}, u32[]{:S(2)}, u32[]{:S(2)}) collective-permute-start(f32[208,1024]{1,0:T(8,128)S(1)} %get-tuple-element.26), channel_id=1, source_target_pairs={{4,0},{8,4},{12,8},{16,12},{20,16},{24,20},{28,24},{32,28},{36,32}... | collective-permute-start | bytes 2555912 | tf_op jit(solution)/shard_map/ppermute | solution.py:435
